TPU v7x, 32 devices: a whole 2x2x4 slice. The times are simulated.
32 devices in a mesh: dp: 16 (over z, y, x), mp: 2 (over core).
Axes of the slice: x: 2, y: 2, z: 4, core: 2. Of those that a mesh axis runs over, the one named last changes fastest.
Arguments:
- inputs: bfloat16 [32768, 4096], P('dp', 'mp'), may hold values from -6 to 6
- cotangents: bfloat16 [32768, 4096], P('dp', 'mp'), may hold values from -6 to 6
- loss_token_mask: int32 [32768], P('dp'), may hold values 0 or 1
- adapter_down_weight: bfloat16 [128, 4096], P(None, 'mp'), may hold values from -0.09375 to 0.09375
- adapter_up_weight: bfloat16 [4096, 128], P('mp'), may hold values from -0.5 to 0.5
- width_projection: bfloat16 [2, 4096, 256], P(None, 'mp'), may hold values from -0.09375 to 0.09375
- rank_projection: bfloat16 [2, 128, 16], replicated, may hold values from -0.5 to 0.5
- targets: float32 [64, 8192], P(None, ('dp', 'mp')), may hold values from -500 to 500
Outputs:
- scores: float32 [128, 64], P('dp')
All inputs are finite; a program needn't handle non-finite values. No bound on the sum of `loss_token_mask` on one device may be relied on, other than what follows from the above.
Results may differ from a plain program's by a relative error of at most 0.0003.
Values sent between devices are 32-bit elements; how exact they have to be, the bound alone decides.
A program may use at most 64 MiB of HBM per device.

v0:
```python
import math
import jax
import jax.numpy as jnp
from jax import lax
from jax.sharding import PartitionSpec as P

SEQ = 256
KP = 256
KQ = 16
FEAT = 8192
adapter_scale = 4.0
epsilon = 1e-06


def on_device(
    inputs,
    cotangents,
    loss_token_mask,
    adapter_down_weight,
    adapter_up_weight,
    width_projection,
    rank_projection,
    targets,
):
    samples = inputs.shape[0] // SEQ
    masked_gradient = cotangents * loss_token_mask.astype(jnp.bfloat16)[:, None]
    cols_first = rank_projection[0].astype(jnp.float32)
    cols_second = rank_projection[1].astype(jnp.float32)
    down_partial_gradient = jnp.dot(
        inputs, adapter_down_weight.T, preferred_element_type=jnp.float32
    )
    up_partial_gradient = jnp.dot(
        masked_gradient, adapter_up_weight, preferred_element_type=jnp.float32
    )
    down_rank_product, up_rank_product = lax.psum(
        (down_partial_gradient, up_partial_gradient), "mp"
    )
    compact_up_gradient = jnp.dot(up_rank_product, cols_first, precision=lax.Precision.HIGHEST)
    compact_down_gradient = jnp.dot(down_rank_product, cols_second, precision=lax.Precision.HIGHEST)
    projected_activations = jnp.dot(
        inputs, width_projection[0], preferred_element_type=jnp.float32
    ).reshape(samples, SEQ, KP)
    projected_masked_gradient = jnp.dot(
        masked_gradient, width_projection[1], preferred_element_type=jnp.float32
    ).reshape(samples, SEQ, KP)
    first_matrix = adapter_scale * jnp.einsum(
        "stk,stq->skq",
        projected_activations,
        compact_up_gradient.reshape(samples, SEQ, KQ),
        precision=lax.Precision.HIGHEST,
    )
    second_matrix = adapter_scale * jnp.einsum(
        "stk,stq->skq",
        projected_masked_gradient,
        compact_down_gradient.reshape(samples, SEQ, KQ),
        precision=lax.Precision.HIGHEST,
    )
    partial_value = jnp.concatenate(
        [first_matrix.reshape(samples, KP * KQ), second_matrix.reshape(samples, KP * KQ)], axis=1
    )
    features = lax.psum(partial_value, "mp")
    every_target = lax.all_gather(targets, ("dp", "mp"), axis=1, tiled=True)
    inner = jnp.dot(features, every_target.T, precision=lax.Precision.HIGHEST)
    sample_squares = jnp.sum(features * features, axis=1)
    target_squares = jnp.sum(every_target * every_target, axis=1)
    sample_rms = jnp.sqrt(sample_squares / FEAT + epsilon)
    target_rms = jnp.sqrt(target_squares / FEAT + epsilon)
    return inner / (math.sqrt(FEAT) * sample_rms[:, None] * target_rms[None, :])


def solution(mesh):
    in_specs = (
        P("dp", "mp"),
        P("dp", "mp"),
        P("dp"),
        P(None, "mp"),
        P("mp", None),
        P(None, "mp", None),
        P(),
        P(None, ("dp", "mp")),
    )
    out_specs = P("dp", None)
    return jax.shard_map(
        on_device, mesh=mesh, in_specs=in_specs, out_specs=out_specs, check_vma=False
    )
```

profile of v0, /device:TPU:0, one launch (start us, length us, event | category | flops | bytes accessed | tf_op | source)
XLA Modules:
  0.0 130.8 jit_solution(16499203396642434931)
XLA Ops:
  7.4 0.0 copy-start
  7.4 0.8 convert_element_type.2
  8.1 7.2 %broadcast_multiply_fusion = bf16[2048,2048]{1,0:T(8,128)(2,1)} fusion(bf16[2048,2048]{1,0:T(8,128)(2,1)} %param.9, bf16[2048]{0:T(1024)(128)(2,1)S(1)} %convert_element_type.2), kind=kLoop, calls=%fused_computation | loop fusion | flops 4194304 | bytes 16781312 | tf_op jit(solution)/shard_map/mul | solution.py:26
  15.4 6.9 %fusion.13 = f32[2048,128]{1,0:T(8,128)} fusion(bf16[2048,2048]{1,0:T(8,128)(2,1)} %param.8, bf16[128,2048]{1,0:T(8,128)(2,1)S(1)} %copy-done), kind=kOutput, calls=%fused_computation.22 | convolution fusion | flops 1073741824 | bytes 9961472 | tf_op jit(solution)/shard_map/dot_general | solution.py:29
  22.3 3.4 %fusion.12 = f32[2048,128]{1,0:T(8,128)} fusion(bf16[2048,2048]{1,0:T(8,128)(2,1)S(1)} %copy-done.1, bf16[2048,128]{1,0:T(8,128)(2,1)S(1)} %copy-done.7), kind=kOutput, calls=%fused_computation.21 | convolution fusion | flops 1073741824 | bytes 9961472 | tf_op jit(solution)/shard_map/dot_general | solution.py:32
  25.7 0.0 all-reduce.6.cloned.1.call-update
  25.7 0.2 all-reduce.4.cloned.1.call-start
  25.9 0.0 copy-start.6
  25.9 6.1 %fusion = f32[8,256,256]{2,1,0:T(8,128)S(1)} fusion(bf16[8,256,2048]{2,1,0:T(8,128)(2,1)} %bitcast.34, bf16[2,2048,256]{2,1,0:T(8,128)(2,1)} %param.13), kind=kOutput, calls=%fused_computation.5 | convolution fusion | flops 2147483648 | bytes 11534336 | tf_op jit(solution)/shard_map/dot_general | solution.py:43
  32.1 0.0 copy-start.5
  32.1 7.8 %fusion.2 = f32[8,256,256]{2,1,0:T(8,128)} fusion(bf16[8,256,2048]{2,1,0:T(8,128)(2,1)} %bitcast.37, bf16[2,2048,256]{2,1,0:T(8,128)(2,1)S(1)} %copy-done.6), kind=kOutput, calls=%fused_computation.7 | convolution fusion | flops 2147483648 | bytes 11534336 | tf_op jit(solution)/shard_map/dot_general | solution.py:40
  39.9 10.0 %all-reduce.6.cloned.1.call-done = (f32[8,256,128]{2,1,0:T(8,128)}, f32[8,256,128]{2,1,0:T(8,128)}) async-done(((f32[8,256,128]{2,1,0:T(8,128)}, f32[8,256,128]{2,1,0:T(8,128)}), (f32[8,256,128]{2,1,0:T(8,128)}, f32[8,256,128]{2,1,0:T(8,128)})) %all-reduce.6.cloned.1.call-update) | async-done | bytes 2097168 | tf_op jit(solution)/shard_map/psum | solution.py:35
  49.8 1.8 %fusion.6 = f32[8,256,16]{1,2,0:T(8,128)S(1)} fusion(f32[8,256,128]{2,1,0:T(8,128)} %get-tuple-element.5, bf16[2,128,16]{1,2,0:T(8,128)(2,1)S(1)} %copy-done.5), kind=kOutput, calls=%fused_computation.13 | convolution fusion | flops 50331648 | bytes 1183744 | tf_op jit(solution)/shard_map/dot_general | solution.py:39
  51.6 1.2 convolution_multiply_fusion
  52.9 0.3 copy.10
  53.2 0.6 reshape.28
  53.8 0.3 copy-done.4
  54.1 0.6 fusion.8
  54.7 2.8 %convolution_multiply_fusion.1 = f32[8,256,16]{1,2,0:T(8,128)S(1)} fusion(f32[8,256,256]{2,1,0:T(8,128)} %fusion.2, f32[8,256,16]{1,2,0:T(8,128)S(1)} %fusion.8), kind=kOutput, calls=%fused_computation.3 | convolution fusion | flops 100696064 | bytes 2359296 | tf_op jit(solution)/shard_map/stk,stq->skq/dot_general | solution.py:46
  57.5 0.3 copy.9
  57.8 0.6 reshape.27
  58.4 0.7 pad_maximum_fusion
  59.2 0.0 all-reduce.4.cloned.1.call-update
  59.2 0.0 all-gather.2.cloned.1.call-start
  59.2 0.5 all-gather.2.cloned.1.call-update
  59.8 19.0 %all-reduce.4.cloned.1.call-done = f32[8,8192]{1,0:T(8,128)} async-done(((f32[8,8192]{1,0:T(8,128)}), f32[8,8192]{1,0:T(8,128)}) %all-reduce.4.cloned.1.call-update) | async-done | bytes 262160 | tf_op jit(solution)/shard_map/psum | solution.py:61
  78.8 1.2 multiply_reduce_fusion.1
  80.0 38.8 %all-gather.2.cloned.1.call-done = f32[64,8192]{1,0:T(8,128)} async-done(((f32[64,256]{1,0:T(8,128)}), f32[64,8192]{1,0:T(8,128)}) %all-gather.2.cloned.1.call-update) | async-done | bytes 2097168 | tf_op jit(solution)/shard_map/all_gather | solution.py:62
  118.8 2.0 %multiply_reduce_fusion = f32[64]{0:T(128)S(1)} fusion(f32[64,8192]{1,0:T(8,128)} %all-gather.2.cloned.1.call-done), kind=kLoop, calls=%fused_computation.1 | loop fusion | flops 1048512 | bytes 2097408 | tf_op jit(solution)/shard_map/reduce_sum | solution.py:65
  120.8 0.0 copy-done.3
  120.8 0.2 copy-done.2
  121.0 2.3 %convolution_divide_fusion = f32[8,64]{1,0:T(8,128)} fusion(f32[8,8192]{1,0:T(8,128)S(1)} %copy-done.3, f32[64,8192]{1,0:T(8,128)S(1)} %copy-done.2, f32[64]{0:T(128)S(1)} %add_sqrt_fusion, f32[8]{0:T(128)S(1)} %sqrt_multiply_fusion), kind=kOutput, calls=%fused_computation.4 | convolution fusion | flops 50332672 | bytes 2361632 | tf_op jit(solution)/shard_map/dot_general | solution.py:63
  (13 shorter events, 0.0 us)
Async XLA Ops:
  7.4 8.0 %copy-start = (bf16[128,2048]{1,0:T(8,128)(2,1)S(1)}, bf16[128,2048]{1,0:T(8,128)(2,1)}, u32[]{:S(2)}) copy-start(bf16[128,2048]{1,0:T(8,128)(2,1)} %param.11) | copy-start | bytes 1572868
  7.4 42.5 %all-reduce.6.cloned.1.call-start = ((), (), s32[]{:S(2)}) async-start(), calls=%async_computation.2 | async-start | bytes 4194304 | tf_op jit(solution)/shard_map/psum | solution.py:35
  15.4 6.9 %copy-start.1 = (bf16[2048,2048]{1,0:T(8,128)(2,1)S(1)}, bf16[2048,2048]{1,0:T(8,128)(2,1)}, u32[]{:S(2)}) copy-start(bf16[2048,2048]{1,0:T(8,128)(2,1)} %broadcast_multiply_fusion) | copy-start | bytes 25165828
  15.4 6.9 %copy-start.7 = (bf16[2048,128]{1,0:T(8,128)(2,1)S(1)}, bf16[2048,128]{1,0:T(8,128)(2,1)}, u32[]{:S(2)}) copy-start(bf16[2048,128]{1,0:T(8,128)(2,1)} %param.12) | copy-start | bytes 1572868
  25.7 53.1 %all-reduce.4.cloned.1.call-start = ((), (), s32[]{:S(2)}) async-start(), calls=%async_computation | async-start | bytes 524288 | tf_op jit(solution)/shard_map/psum | solution.py:61
  25.9 6.1 %copy-start.6 = (bf16[2,2048,256]{2,1,0:T(8,128)(2,1)S(1)}, bf16[2,2048,256]{2,1,0:T(8,128)(2,1)}, u32[]{:S(2)}) copy-start(bf16[2,2048,256]{2,1,0:T(8,128)(2,1)} %param.13) | copy-start | bytes 6291460
  32.1 17.8 %copy-start.5 = (bf16[2,128,16]{1,2,0:T(8,128)(2,1)S(1)}, bf16[2,128,16]{1,2,0:T(8,128)(2,1)}, u32[]{:S(2)}) copy-start(bf16[2,128,16]{1,2,0:T(8,128)(2,1)} %param.14) | copy-start | bytes 24580
  52.8 1.2 copy-start.4
  59.2 59.6 %all-gather.2.cloned.1.call-start = ((), (), s32[]{:S(2)}) async-start(), calls=%async_computation.1 | async-start | bytes 2162688 | tf_op jit(solution)/shard_map/all_gather | solution.py:62
  78.8 42.0 %copy-start.3 = (f32[8,8192]{1,0:T(8,128)S(1)}, f32[8,8192]{1,0:T(8,128)}, u32[]{:S(2)}) copy-start(f32[8,8192]{1,0:T(8,128)} %all-reduce.4.cloned.1.call-done) | copy-start | bytes 786436
  118.8 2.2 %copy-start.2 = (f32[64,8192]{1,0:T(8,128)S(1)}, f32[64,8192]{1,0:T(8,128)}, u32[]{:S(2)}) copy-start(f32[64,8192]{1,0:T(8,128)} %all-gather.2.cloned.1.call-done) | copy-start | bytes 6291460
Sparse Core Ops, SparseCore 0:
  25.8 23.9 all-reduce.5
  59.3 19.4 all-reduce.3
Sparse Core Ops, SparseCore 1:
  62.6 56.1 all-gather.1
where the time goes:
time: 131 us
  waiting for transfers between devices  68.3 us (52%)
  matrix products  32.9 us (25%)
  between operations  14.9 us (11%)
  other arithmetic  11.9 us (9%)
  local copies, waits for them, and re-layouts  2.42 us (2%)
    all_gather x1, waiting for transfers between devices, on_device(): every_target = lax.all_gather(targets, ('dp', 'mp'), axis=1, tiled=True)  38.8 us
    psum x1, waiting for transfers between devices, on_device(): features = lax.psum(partial_value, 'mp')  19 us
    psum x1, waiting for transfers between devices, on_device(): lax.psum((down_partial_gradient, up_partial_gradient), 'mp')  9.98 us
    dot_general x1, matrix products, on_device(): jnp.dot(inputs, width_projection[0], preferred_element_type=jnp.float32)  7.79 us
    mul x1, other arithmetic, on_device(): masked_gradient = cotangents * loss_token_mask.astype(jnp.bfloat16)[:, None]  7.23 us
    dot_general x1, matrix products, on_device(): jnp.dot(inputs, adapter_down_weight.T, preferred_element_type=jnp.float32)  6.87 us
    dot_general x1, matrix products, on_device(): jnp.dot(masked_gradient, width_projection[1], preferred_element_type=jnp....  6.11 us
    dot_general x1, matrix products, on_device(): jnp.dot(masked_gradient, adapter_up_weight, preferred_element_type=jnp.fl...  3.41 us
  transfers between devices with their start and end apart: 3, of which 3 were waited for; matrix products, arithmetic and copies ran while one was open for 12% of the time, Pallas kernels for 0%

commit v1 on v0

--- a/solution.py
+++ b/solution.py
@@ -59,7 +59,14 @@
         [first_matrix.reshape(samples, KP * KQ), second_matrix.reshape(samples, KP * KQ)], axis=1
     )
     features = lax.psum(partial_value, "mp")
-    every_target = lax.all_gather(targets, ("dp", "mp"), axis=1, tiled=True)
+    ways, here = (lax.axis_size(("dp", "mp")), lax.axis_index(("dp", "mp")))
+    every_target, reach = (targets, 1)
+    while reach < ways:
+        theirs = lax.ppermute(every_target, ("dp", "mp"), [(d, d ^ reach) for d in range(ways)])
+        mine_first = jnp.concatenate([every_target, theirs], axis=1)
+        theirs_first = jnp.concatenate([theirs, every_target], axis=1)
+        every_target = jnp.where(here & reach == 0, mine_first, theirs_first)
+        reach = 2 * reach
     inner = jnp.dot(features, every_target.T, precision=lax.Precision.HIGHEST)
     sample_squares = jnp.sum(features * features, axis=1)
     target_squares = jnp.sum(every_target * every_target, axis=1)

time: 131 us -> 116 us (0.89)
  waiting for transfers between devices: 68.3 us -> 38.2 us
  starting transfers between devices: 0.27 us -> 9.16 us
  matrix products: 32.9 us -> 40.9 us
  between operations: 14.9 us -> 13.5 us
    all_gather x1 -> x0, waiting for transfers between devices: 38.8 us -> none  [on_device(): every_target = lax.all_gather(targets, ('dp', 'mp'), axis=1, tiled=True)]
    ppermute x0 -> x5, waiting for transfers between devices: none -> 38.2 us  [on_device(): lax.ppermute(every_target, ('dp', 'mp'), [(d, d ^ reach) for d in range(w...]
    psum x1, waiting for transfers between devices: 19 us -> 0.02 us  [on_device(): features = lax.psum(partial_value, 'mp')]
    psum x1, waiting for transfers between devices: 9.98 us -> 0.01 us  [on_device(): lax.psum((down_partial_gradient, up_partial_gradient), 'mp')]
    ppermute x0 -> x5, starting transfers between devices: none -> 8.93 us  [on_device(): lax.ppermute(every_target, ('dp', 'mp'), [(d, d ^ reach) for d in range(w...]
    dot_general x1, matrix products: 3.41 us -> 6.71 us  [on_device(): jnp.dot(masked_gradient, adapter_up_weight, preferred_element_type=jnp.fl...]
    dot_general x1, matrix products: 2.33 us -> 3.99 us  [on_device(): inner = jnp.dot(features, every_target.T, precision=lax.Precision.HIGHEST)]
    dot_general x1, matrix products: 1.21 us -> 2.8 us  [on_device(): jnp.einsum('stk,stq->skq', projected_masked_gradient, compact_down_gradie...]
  transfers between devices with their start and end apart: 3 -> 7, of which waited for: 3 -> 2; matrix products, arithmetic and copies ran while one was open for 12% -> 43% of each run, Pallas kernels for 0% -> 0%
where the time goes in v1:
time: 116 us
  matrix products  40.9 us (35%)
  waiting for transfers between devices  38.2 us (33%)
  between operations  13.5 us (12%)
  other arithmetic  11.9 us (10%)
  starting transfers between devices  9.16 us (8%)
  local copies, waits for them, and re-layouts  1.93 us (2%)
    ppermute x5, waiting for transfers between devices, on_device(): lax.ppermute(every_target, ('dp', 'mp'), [(d, d ^ reach) for d in range(w...  38.2 us
    ppermute x5, starting transfers between devices, on_device(): lax.ppermute(every_target, ('dp', 'mp'), [(d, d ^ reach) for d in range(w...  8.93 us
    mul x1, other arithmetic, on_device(): masked_gradient = cotangents * loss_token_mask.astype(jnp.bfloat16)[:, None]  7.22 us
    dot_general x1, matrix products, on_device(): jnp.dot(masked_gradient, width_projection[1], preferred_element_type=jnp....  7.09 us
    dot_general x1, matrix products, on_device(): jnp.dot(inputs, width_projection[0], preferred_element_type=jnp.float32)  7.09 us
    dot_general x1, matrix products, on_device(): jnp.dot(inputs, adapter_down_weight.T, preferred_element_type=jnp.float32)  6.84 us
    dot_general x1, matrix products, on_device(): jnp.dot(masked_gradient, adapter_up_weight, preferred_element_type=jnp.fl...  6.71 us
    dot_general x1, matrix products, on_device(): inner = jnp.dot(features, every_target.T, precision=lax.Precision.HIGHEST)  3.99 us
  transfers between devices with their start and end apart: 7, of which 2 were waited for; matrix products, arithmetic and copies ran while one was open for 43% of the time, Pallas kernels for 0%

profile of v1, /device:TPU:0, one launch (start us, length us, event | category | flops | bytes accessed | tf_op | source)
XLA Modules:
  0.0 115.6 jit_solution(12106173265976694086)
XLA Ops:
  6.5 0.5 collective-permute-start
  7.0 0.7 convert_element_type.2
  7.7 7.2 %broadcast_multiply_fusion = bf16[2048,2048]{1,0:T(8,128)(2,1)} fusion(bf16[2048,2048]{1,0:T(8,128)(2,1)} %param.9, bf16[2048]{0:T(1024)(128)(2,1)S(1)} %convert_element_type.2), kind=kLoop, calls=%fused_computation | loop fusion | flops 4194304 | bytes 16781312 | tf_op jit(solution)/shard_map/mul | solution.py:26
  14.9 6.8 %fusion.17 = f32[2048,128]{1,0:T(8,128)} fusion(bf16[2048,2048]{1,0:T(8,128)(2,1)} %param.8, bf16[128,2048]{1,0:T(8,128)(2,1)S(1)} %copy-done), kind=kOutput, calls=%fused_computation.30 | convolution fusion | flops 1073741824 | bytes 9961472 | tf_op jit(solution)/shard_map/dot_general | solution.py:29
  21.8 0.0 collective-permute-done
  21.8 2.6 %collective-permute-start.1 = (f32[64,512]{1,0:T(8,128)S(1)}, f32[64,512]{1,0:T(8,128)S(1)}, u32[]{:S(2)}, u32[]{:S(2)}) collective-permute-start(f32[64,512]{1,0:T(8,128)S(1)} %maximum_select_fusion.7), channel_id=1, source_target_pairs={{0,2},{1,3},{2,0},{3,1},{4,6},{5,7},{6,4},{7,5},{8,10},{9,11},{10,... | collective-permute-start | bytes 393224 | tf_op jit(solution)/shard_map/ppermute | solution.py:65
  24.4 6.7 %fusion.16 = f32[2048,128]{1,0:T(8,128)} fusion(bf16[2048,2048]{1,0:T(8,128)(2,1)} %broadcast_multiply_fusion, bf16[2048,128]{1,0:T(8,128)(2,1)S(1)} %copy-done.4), kind=kOutput, calls=%fused_computation.29 | convolution fusion | flops 1073741824 | bytes 9961472 | tf_op jit(solution)/shard_map/dot_general | solution.py:32
  31.1 0.0 all-reduce.6.cloned.1.call-update
  31.1 0.2 all-reduce.4.cloned.1.call-start
  31.4 1.6 %collective-permute-start.2 = (f32[64,1024]{1,0:T(8,128)S(1)}, f32[64,1024]{1,0:T(8,128)S(1)}, u32[]{:S(2)}, u32[]{:S(2)}) collective-permute-start(f32[64,1024]{1,0:T(8,128)S(1)} %maximum_select_fusion.6), channel_id=1, source_target_pairs={{0,4},{1,5},{2,6},{3,7},{4,0},{5,1},{6,2},{7,3},{8,12},{9,13},{10,... | collective-permute-start | bytes 786440 | tf_op jit(solution)/shard_map/ppermute | solution.py:65
  33.0 7.1 %fusion.2 = f32[8,256,256]{2,1,0:T(8,128)} fusion(bf16[8,256,2048]{2,1,0:T(8,128)(2,1)} %bitcast.33, bf16[2,2048,256]{2,1,0:T(8,128)(2,1)S(1)} %copy-done.3), kind=kOutput, calls=%fused_computation.8 | convolution fusion | flops 2147483648 | bytes 11534336 | tf_op jit(solution)/shard_map/dot_general | solution.py:43
  40.1 0.0 collective-permute-done.2
  40.1 1.6 %collective-permute-start.3 = (f32[64,2048]{1,0:T(8,128)S(1)}, f32[64,2048]{1,0:T(8,128)S(1)}, u32[]{:S(2)}, u32[]{:S(2)}) collective-permute-start(f32[64,2048]{1,0:T(8,128)S(1)} %maximum_select_fusion.5), channel_id=1, source_target_pairs={{0,8},{1,9},{2,10},{3,11},{4,12},{5,13},{6,14},{7,15},{8,0},{9,1},... | collective-permute-start | bytes 1572872 | tf_op jit(solution)/shard_map/ppermute | solution.py:65
  41.8 7.1 %fusion.4 = f32[8,256,256]{2,1,0:T(8,128)} fusion(bf16[8,256,2048]{2,1,0:T(8,128)(2,1)} %bitcast.36, bf16[2,2048,256]{2,1,0:T(8,128)(2,1)S(1)} %copy-done.3), kind=kOutput, calls=%fused_computation.10 | convolution fusion | flops 2147483648 | bytes 11534336 | tf_op jit(solution)/shard_map/dot_general | solution.py:40
  48.9 5.1 %collective-permute-done.3 = f32[64,2048]{1,0:T(8,128)S(1)} collective-permute-done((f32[64,2048]{1,0:T(8,128)S(1)}, f32[64,2048]{1,0:T(8,128)S(1)}, u32[]{:S(2)}, u32[]{:S(2)}) %collective-permute-start.3) | collective-permute-done | bytes 524320 | tf_op jit(solution)/shard_map/ppermute | solution.py:65
  53.9 0.1 maximum_select_fusion.4
  54.1 2.6 %collective-permute-start.4 = (f32[64,4096]{1,0:T(8,128)S(1)}, f32[64,4096]{1,0:T(8,128)}, u32[]{:S(2)}, u32[]{:S(2)}) collective-permute-start(f32[64,4096]{1,0:T(8,128)S(1)} %maximum_select_fusion.4), channel_id=1, source_target_pairs={{0,16},{1,17},{2,18},{3,19},{4,20},{5,21},{6,22},{7,23},{8,24},{9,... | collective-permute-start | bytes 3145736 | tf_op jit(solution)/shard_map/ppermute | solution.py:65
  56.7 1.8 %fusion.9 = f32[8,256,16]{1,2,0:T(8,128)S(1)} fusion(f32[8,256,128]{2,1,0:T(8,128)} %get-tuple-element.5, bf16[2,128,16]{1,2,0:T(8,128)(2,1)S(1)} %copy-done.2), kind=kOutput, calls=%fused_computation.20 | convolution fusion | flops 50331648 | bytes 1183744 | tf_op jit(solution)/shard_map/dot_general | solution.py:39
  58.5 2.8 %convolution_multiply_fusion = f32[8,256,16]{1,2,0:T(8,128)S(1)} fusion(f32[8,256,256]{2,1,0:T(8,128)} %fusion.2, f32[8,256,16]{1,2,0:T(8,128)S(1)} %fusion.9), kind=kOutput, calls=%fused_computation.4 | convolution fusion | flops 100696064 | bytes 2359296 | tf_op jit(solution)/shard_map/stk,stq->skq/dot_general | solution.py:52
  61.3 0.3 copy.10
  61.7 0.6 reshape.28
  62.3 1.8 %fusion.11 = f32[8,256,16]{1,2,0:T(8,128)S(1)} fusion(f32[8,256,128]{2,1,0:T(8,128)} %get-tuple-element.6, bf16[2,128,16]{1,2,0:T(8,128)(2,1)S(1)} %copy-done.2), kind=kOutput, calls=%fused_computation.22 | convolution fusion | flops 50331648 | bytes 1183744 | tf_op jit(solution)/shard_map/dot_general | solution.py:38
  64.1 2.8 %convolution_multiply_fusion.1 = f32[8,256,16]{1,2,0:T(8,128)S(1)} fusion(f32[8,256,256]{2,1,0:T(8,128)} %fusion.4, f32[8,256,16]{1,2,0:T(8,128)S(1)} %fusion.11), kind=kOutput, calls=%fused_computation.5 | convolution fusion | flops 100696064 | bytes 2359296 | tf_op jit(solution)/shard_map/stk,stq->skq/dot_general | solution.py:46
  66.9 0.3 copy.9
  67.2 0.6 reshape.27
  67.9 0.7 pad_maximum_fusion
  68.6 0.0 all-reduce.4.cloned.1.call-update
  68.6 33.1 %collective-permute-done.4 = f32[64,4096]{1,0:T(8,128)} collective-permute-done((f32[64,4096]{1,0:T(8,128)S(1)}, f32[64,4096]{1,0:T(8,128)}, u32[]{:S(2)}, u32[]{:S(2)}) %collective-permute-start.4) | collective-permute-done | bytes 1048608 | tf_op jit(solution)/shard_map/ppermute | solution.py:65
  101.7 1.9 %multiply_reduce_fusion = f32[64]{0:T(128)S(1)} fusion(f32[64,4096]{1,0:T(8,128)S(1)} %maximum_select_fusion.4, f32[64,4096]{1,0:T(8,128)} %collective-permute-done.4, pred[]{:T(512)S(6)} %eq.15), kind=kLoop, calls=%fused_computation.2 | loop fusion | flops 2621376 | bytes 2097409 | tf_op jit(solution)/shard_map/reduce_sum | solution.py:72
  103.6 0.0 all-reduce.4.cloned.1.call-done
  103.7 1.1 multiply_reduce_fusion.1
  104.8 4.0 %fusion.1 = f32[8,64]{1,0:T(8,128)} fusion(f32[8,8192]{1,0:T(8,128)} %all-reduce.4.cloned.1.call-done, f32[64,4096]{1,0:T(8,128)} %collective-permute-done.4, f32[64,4096]{1,0:T(8,128)S(1)} %maximum_select_fusion.4, pred[]{:T(512)S(6)} %eq.15, f32[64]{0:T(128)S(1)} %add_sqrt_fusion, f32[8]{0:T(128)S(1)} %sqrt_multiply_fusion), kind=kOutput, calls=%fused_computation.6 | convolution fusion | flops 51905536 | bytes 2361633 | tf_op jit(solution)/shard_map/dot_general | solution.py:70
  (18 shorter events, 0.1 us)
Async XLA Ops:
  6.5 8.4 %copy-start = (bf16[128,2048]{1,0:T(8,128)(2,1)S(1)}, bf16[128,2048]{1,0:T(8,128)(2,1)}, u32[]{:S(2)}) copy-start(bf16[128,2048]{1,0:T(8,128)(2,1)} %param.11) | copy-start | bytes 1572868
  6.5 50.2 %all-reduce.6.cloned.1.call-start = ((), (), s32[]{:S(2)}) async-start(), calls=%async_computation.1 | async-start | bytes 4194304 | tf_op jit(solution)/shard_map/psum | solution.py:35
  6.5 15.2 %collective-permute-start = (f32[64,256]{1,0:T(8,128)}, f32[64,256]{1,0:T(8,128)S(1)}, u32[]{:S(2)}, u32[]{:S(2)}) collective-permute-start(f32[64,256]{1,0:T(8,128)} %param.15), channel_id=1, source_target_pairs={{0,1},{1,0},{2,3},{3,2},{4,5},{5,4},{6,7},{7,6},{8,9},{9,8},{10,11... | collective-permute-start | bytes 196616 | tf_op jit(solution)/shard_map/ppermute | solution.py:65
  14.9 6.9 %copy-start.1 = (f32[64,256]{1,0:T(8,128)S(1)}, f32[64,256]{1,0:T(8,128)}, u32[]{:S(2)}) copy-start(f32[64,256]{1,0:T(8,128)} %param.15) | copy-start | bytes 196612
  14.9 9.5 %copy-start.4 = (bf16[2048,128]{1,0:T(8,128)(2,1)S(1)}, bf16[2048,128]{1,0:T(8,128)(2,1)}, u32[]{:S(2)}) copy-start(bf16[2048,128]{1,0:T(8,128)(2,1)} %param.12) | copy-start | bytes 1572868
  21.8 9.6 %collective-permute-start.1 = (f32[64,512]{1,0:T(8,128)S(1)}, f32[64,512]{1,0:T(8,128)S(1)}, u32[]{:S(2)}, u32[]{:S(2)}) collective-permute-start(f32[64,512]{1,0:T(8,128)S(1)} %maximum_select_fusion.7), channel_id=1, source_target_pairs={{0,2},{1,3},{2,0},{3,1},{4,6},{5,7},{6,4},{7,5},{8,10},{9,11},{10,... | collective-permute-start | bytes 393224 | tf_op jit(solution)/shard_map/ppermute | solution.py:65
  31.1 1.9 %copy-start.3 = (bf16[2,2048,256]{2,1,0:T(8,128)(2,1)S(1)}, bf16[2,2048,256]{2,1,0:T(8,128)(2,1)}, u32[]{:S(2)}) copy-start(bf16[2,2048,256]{2,1,0:T(8,128)(2,1)} %param.13) | copy-start | bytes 6291460
  31.1 72.5 %all-reduce.4.cloned.1.call-start = ((), (), s32[]{:S(2)}) async-start(), calls=%async_computation | async-start | bytes 524288 | tf_op jit(solution)/shard_map/psum | solution.py:61
  31.4 8.7 %collective-permute-start.2 = (f32[64,1024]{1,0:T(8,128)S(1)}, f32[64,1024]{1,0:T(8,128)S(1)}, u32[]{:S(2)}, u32[]{:S(2)}) collective-permute-start(f32[64,1024]{1,0:T(8,128)S(1)} %maximum_select_fusion.6), channel_id=1, source_target_pairs={{0,4},{1,5},{2,6},{3,7},{4,0},{5,1},{6,2},{7,3},{8,12},{9,13},{10,... | collective-permute-start | bytes 786440 | tf_op jit(solution)/shard_map/ppermute | solution.py:65
  40.1 13.8 %collective-permute-start.3 = (f32[64,2048]{1,0:T(8,128)S(1)}, f32[64,2048]{1,0:T(8,128)S(1)}, u32[]{:S(2)}, u32[]{:S(2)}) collective-permute-start(f32[64,2048]{1,0:T(8,128)S(1)} %maximum_select_fusion.5), channel_id=1, source_target_pairs={{0,8},{1,9},{2,10},{3,11},{4,12},{5,13},{6,14},{7,15},{8,0},{9,1},... | collective-permute-start | bytes 1572872 | tf_op jit(solution)/shard_map/ppermute | solution.py:65
  48.9 7.9 %copy-start.2 = (bf16[2,128,16]{1,2,0:T(8,128)(2,1)S(1)}, bf16[2,128,16]{1,2,0:T(8,128)(2,1)}, u32[]{:S(2)}) copy-start(bf16[2,128,16]{1,2,0:T(8,128)(2,1)} %param.14) | copy-start | bytes 24580
  54.1 47.6 %collective-permute-start.4 = (f32[64,4096]{1,0:T(8,128)S(1)}, f32[64,4096]{1,0:T(8,128)}, u32[]{:S(2)}, u32[]{:S(2)}) collective-permute-start(f32[64,4096]{1,0:T(8,128)S(1)} %maximum_select_fusion.4), channel_id=1, source_target_pairs={{0,16},{1,17},{2,18},{3,19},{4,20},{5,21},{6,22},{7,23},{8,24},{9,... | collective-permute-start | bytes 3145736 | tf_op jit(solution)/shard_map/ppermute | solution.py:65
Sparse Core Ops, SparseCore 0:
  31.3 21.6 all-reduce.5
  68.7 16.5 all-reduce.3
